TPU v7x, 32 devices: a whole 2x2x4 slice. The times are simulated.
32 devices in a mesh: shot: 2 (over y), gx: 4 (over z), gy: 4 (over x, core).
Axes of the slice: x: 2, y: 2, z: 4, core: 2. Of those that a mesh axis runs over, the one named last changes fastest.
Arguments:
- source_prev: float32 [64, 32, 320], P(('shot', 'gx'), 'gy'), parts along dimension 0, may hold values from -0.6 to 0.6
- source_now: float32 [64, 32, 320], P(('shot', 'gx'), 'gy'), parts along dimension 0, may hold values from -0.6 to 0.6
- receiver_prev: float32 [64, 32, 320], P(('shot', 'gx'), 'gy'), parts along dimension 0, may hold values from -6 to 6
- receiver_now: float32 [64, 32, 320], P(('shot', 'gx'), 'gy'), parts along dimension 0, may hold values from -6 to 6
- speed_squared: float32 [64, 32, 320], P(('shot', 'gx'), 'gy'), parts along dimension 0, may hold values from 0.05 to 0.18
- wavelet: float32 [20], P('shot'), parts along dimension 0, may hold values from -40 to 40
- source_cell: int32 [2], P('shot'), parts along dimension 0, may hold values from 0 to 327679
- traces: float32 [20, 1024], P('shot', ('gx', 'gy')), parts along dimension 0, may hold values from -18 to 18
- receiver_cells: int32 [2, 1024], P('shot', ('gx', 'gy')), parts along dimension 0, may hold values from 0 to 1023
- plan: int32 [8], P('shot'), parts along dimension 0, may hold values from 0 to 9, as said below
- stored_snapshots: bfloat16 [8, 32, 32, 320], P('shot', 'gx', 'gy'), parts along dimension 0, may hold values from -6 to 6
- image_before: float32 [64, 32, 320], P(('shot', 'gx'), 'gy'), parts along dimension 0, may hold values from -6 to 6
Outputs:
- new_source_prev: float32 [64, 32, 320], P(('shot', 'gx'), 'gy'), parts along dimension 0
- new_source_now: float32 [64, 32, 320], P(('shot', 'gx'), 'gy'), parts along dimension 0
- new_receiver_prev: float32 [64, 32, 320], P(('shot', 'gx'), 'gy'), parts along dimension 0
- new_receiver_now: float32 [64, 32, 320], P(('shot', 'gx'), 'gy'), parts along dimension 0
- snapshots: bfloat16 [8, 32, 32, 320], P('shot', 'gx', 'gy'), parts along dimension 0
- image: float32 [64, 32, 320], P(('shot', 'gx'), 'gy'), parts along dimension 0
There are 2 independent parts, one for each index of `shot`. A program takes and returns all parts, laid end to end along the dimension named above; each array names one. Nothing has to cross between parts.
Inputs may be any that keep to these rules, and one draw needn't show every extreme that they name: `plan`: 4 different steps in increasing order; the first is 0 and the last is 9.
All inputs are finite; a program needn't handle non-finite values.
Results may differ from a plain program's by a relative error of at most 0.001.
Values sent between devices are 32-bit elements; how exact they have to be, the bound alone decides.
A program may use at most 64 MiB of HBM per device.

v0:
```python
import jax
import jax.numpy as jnp
from jax import lax
from jax.sharding import PartitionSpec as P

STENCIL_COEFFS = (-205.0 / 72.0, 8.0 / 5.0, -1.0 / 5.0, 8.0 / 315.0, -1.0 / 560.0)


def with_halo(block, sides, width):
    for axis, dim in sides:
        count = lax.axis_size(axis)
        forward = [(i, i + 1) for i in range(count - 1)]
        backward = [(target, source) for source, target in forward]
        low = lax.ppermute(
            lax.slice_in_dim(block, block.shape[dim] - width, None, axis=dim), axis, forward
        )
        high = lax.ppermute(lax.slice_in_dim(block, 0, width, axis=dim), axis, backward)
        block = jnp.concatenate([low, block, high], axis=dim)
    return block


def stencil(padded):
    span_x = padded.shape[0] - 8
    span_y = padded.shape[1] - 8
    depth_cells = padded.shape[2]
    deepened = jnp.pad(padded, ((0, 0), (0, 0), (4, 4)))

    def window(shift_x, shift_y, shift_z):
        return deepened[
            4 + shift_x : 4 + shift_x + span_x,
            4 + shift_y : 4 + shift_y + span_y,
            4 + shift_z : 4 + shift_z + depth_cells,
        ]

    summed = 3.0 * STENCIL_COEFFS[0] * window(0, 0, 0)
    for distance in range(1, 5):
        neighbours = window(distance, 0, 0) + window(-distance, 0, 0)
        neighbours = neighbours + window(0, distance, 0) + window(0, -distance, 0)
        neighbours = neighbours + window(0, 0, distance) + window(0, 0, -distance)
        summed = summed + STENCIL_COEFFS[distance] * neighbours
    return summed


def body(
    source_prev,
    source_now,
    receiver_prev,
    receiver_now,
    speed_squared,
    wavelet,
    source_cell,
    traces,
    receiver_cells,
    plan,
    stored_snapshots,
    image_before,
):
    block_x, block_y, depth_cells = source_now.shape
    grid_y = block_y * lax.axis_size("gy")
    start_x = lax.axis_index("gx") * block_x
    start_y = lax.axis_index("gy") * block_y
    total_steps = wavelet.shape[0]
    slot_count = plan.shape[0]
    border = 0
    span_x = block_x + 2 * border
    span_y = block_y + 2 * border
    plane_cells = span_x * span_y
    values = lax.all_gather(traces, ("gx", "gy"), axis=1, tiled=True)
    cell_ids = lax.all_gather(receiver_cells, ("gx", "gy"), axis=1, tiled=True)
    cell_ids = cell_ids[0]
    local_x = cell_ids // grid_y - (start_x - border)
    local_y = cell_ids % grid_y - (start_y - border)
    in_block = (local_x >= 0) & (local_x < span_x) & (local_y >= 0) & (local_y < span_y)
    local_cell = jnp.where(in_block, local_x * span_y + local_y, plane_cells)
    injected = (
        jnp.zeros((total_steps, plane_cells), jnp.float32)
        .at[:, local_cell]
        .add(values, mode="drop")
    )
    injected = injected.reshape(total_steps, span_x, span_y)
    snapshots = jnp.zeros(stored_snapshots.shape, jnp.bfloat16)
    imaged = image_before
    along_x = start_x - 0 + lax.broadcasted_iota(jnp.int32, (block_x + 2 * 0, 1, 1), 0)
    along_y = start_y - 0 + lax.broadcasted_iota(jnp.int32, (1, block_y + 2 * 0, 1), 1)
    along_x, along_y = (along_x, along_y)
    along_z = lax.broadcasted_iota(jnp.int32, (1, 1, depth_cells), 2)
    cell_id = source_cell[0]
    matches = (along_x == cell_id // (grid_y * depth_cells)) & (
        along_y == cell_id // depth_cells % grid_y
    )
    matches = matches & (along_z == cell_id % depth_cells)
    source_core = matches.astype(jnp.float32)
    source_before, source_field = (source_prev, source_now)
    receiver_before, receiver_field = (receiver_prev, receiver_now)
    for step_index in range(total_steps):
        back_time = total_steps - 1 - step_index
        padded = with_halo(jnp.stack([source_field, receiver_field]), (("gx", 1), ("gy", 2)), 4)
        source_spread = stencil(padded[0]) + wavelet[step_index] * source_core
        receiver_spread = stencil(padded[1]).at[:, :, 0].add(injected[back_time])
        source_latest = 2.0 * source_field - source_before + speed_squared * source_spread
        receiver_latest = 2.0 * receiver_field - receiver_before + speed_squared * receiver_spread
        source_before, source_field = (source_field, source_latest)
        receiver_before, receiver_field = (receiver_field, receiver_latest)
        record_matches = plan == step_index
        snapshots = jnp.where(
            record_matches[:, None, None, None], source_field.astype(jnp.bfloat16)[None], snapshots
        )
        correlate_matches = plan == back_time
        slot_index = jnp.sum(
            jnp.where(correlate_matches, jnp.arange(slot_count, dtype=jnp.int32), 0)
        )
        present = jnp.any(correlate_matches)
        snapshot = lax.dynamic_index_in_dim(stored_snapshots, slot_index, 0, keepdims=False).astype(
            jnp.float32
        )
        imaged = imaged + jnp.where(present, snapshot * receiver_field, 0.0)
    source_last, source_final = (source_before, source_field)
    previous, current = (receiver_before, receiver_field)
    return (source_last, source_final, previous, current, snapshots, imaged)


def solution(mesh):
    placed = (
        P(("shot", "gx"), "gy", None),
        P(("shot", "gx"), "gy", None),
        P(("shot", "gx"), "gy", None),
        P(("shot", "gx"), "gy", None),
        P(("shot", "gx"), "gy", None),
        P("shot"),
        P("shot"),
        P("shot", ("gx", "gy")),
        P("shot", ("gx", "gy")),
        P("shot"),
        P("shot", "gx", "gy", None),
        P(("shot", "gx"), "gy", None),
    )
    return jax.shard_map(
        body,
        mesh=mesh,
        in_specs=placed,
        out_specs=(
            P(("shot", "gx"), "gy", None),
            P(("shot", "gx"), "gy", None),
            P(("shot", "gx"), "gy", None),
            P(("shot", "gx"), "gy", None),
            P("shot", "gx", "gy", None),
            P(("shot", "gx"), "gy", None),
        ),
        check_vma=False,
    )
```

profile of v0, /device:TPU:18, one launch (start us, length us, event | category | flops | bytes accessed | tf_op | source)
XLA Modules:
  0.0 254.4 jit_solution(9579591347282151355)
XLA Ops:
  1.6 2.5 collective-permute-start.1
  4.1 3.5 %collective-permute-start = (f32[2,4,8,320]{3,2,1,0:T(8,128)S(1)}, f32[2,4,8,320]{3,2,1,0:T(8,128)S(1)}, u32[]{:S(2)}, u32[]{:S(2)}) collective-permute-start(f32[2,4,8,320]{3,2,1,0:T(8,128)S(1)} %get-tuple-element.250), channel_id=1, source_target_pairs={{0,4},{4,8},{8,12},{1,5},{5,9},{9,13},{2,6},{6,10},{10,14},{3,7},{... | collective-permute-start | bytes 245768 | tf_op jit(solution)/shard_map/ppermute | solution.py:14
  9.7 9.4 %all-reduce.20 = s32[1024]{0:T(1024)S(1)} all-reduce(s32[1024]{0:T(1024)S(1)} %bitcast_dynamic-update-slice_fusion), channel_id=1, replica_groups=mesh['shot'=2,'gx'=4,'gy'=4] {'gx','gy'}, use_global_device_ids=true, to_apply=%add.20 | all-reduce | flops 1024 | bytes 8192
  21.3 2.4 collective-permute-start.2
  23.8 15.2 %all-gather = f32[16,64,10]{1,2,0:T(8,128)S(1)} all-gather(f32[1,64,10]{1,2,0:T(8,128)S(1)} %bitcast.208), channel_id=1, replica_groups=mesh['shot'=2,'gx'=4,'gy'=4] {'gx','gy'}, dimensions={0}, use_global_device_ids=true | all-gather | bytes 43520 | tf_op jit(solution)/shard_map/all_gather | solution.py:68
  39.2 6.0 %scatter_custom_fusion = f32[10,64]{0,1:T(8,128)S(1)} fusion(s32[1024]{0:T(1024)S(1)} %bitcast.209, f32[1024,10]{1,0:T(8,128)S(1)} %bitcast.206, f32[]{:T(128)} %constant.323.clone.1), kind=kCustom, calls=%fused_computation.926 | custom fusion | flops 10240 | bytes 2564 | tf_op jit(solution)/shard_map/scatter-add | solution.py:78
  49.3 3.3 %collective-permute-start.5 = (f32[2,4,8,320]{3,2,1,0:T(8,128)S(1)}, f32[2,4,8,320]{3,2,1,0:T(8,128)S(1)}, u32[]{:S(2)}, u32[]{:S(2)}) collective-permute-start(f32[2,4,8,320]{3,2,1,0:T(8,128)S(1)} %get-tuple-element.249), channel_id=1, source_target_pairs={{4,0},{8,4},{12,8},{5,1},{9,5},{13,9},{6,2},{10,6},{14,10},{7,3},{... | collective-permute-start | bytes 245768 | tf_op jit(solution)/shard_map/ppermute | solution.py:17
  52.6 2.6 %collective-permute-start.4 = (f32[2,4,8,320]{3,2,1,0:T(8,128)S(1)}, f32[2,4,8,320]{3,2,1,0:T(8,128)S(1)}, u32[]{:S(2)}, u32[]{:S(2)}) collective-permute-start(f32[2,4,8,320]{3,2,1,0:T(8,128)S(1)} %get-tuple-element.248), channel_id=1, source_target_pairs={{0,4},{4,8},{8,12},{1,5},{5,9},{9,13},{2,6},{6,10},{10,14},{3,7},{... | collective-permute-start | bytes 245768 | tf_op jit(solution)/shard_map/ppermute | solution.py:14
  56.3 4.3 %collective-permute-done.4 = f32[2,4,8,320]{3,2,1,0:T(8,128)S(1)} collective-permute-done((f32[2,4,8,320]{3,2,1,0:T(8,128)S(1)}, f32[2,4,8,320]{3,2,1,0:T(8,128)S(1)}, u32[]{:S(2)}, u32[]{:S(2)}) %collective-permute-start.4) | collective-permute-done | bytes 81952 | tf_op jit(solution)/shard_map/ppermute | solution.py:14
  60.7 3.6 %collective-permute-start.7 = (f32[2,16,4,320]{3,1,2,0:T(8,128)S(1)}, f32[2,16,4,320]{3,1,2,0:T(8,128)S(1)}, u32[]{:S(2)}, u32[]{:S(2)}) collective-permute-start(f32[2,16,4,320]{3,1,2,0:T(8,128)S(1)} %copy.731), channel_id=1, source_target_pairs={{1,0},{2,1},{3,2},{5,4},{6,5},{7,6},{9,8},{10,9},{11,10},{13,12},{... | collective-permute-start | bytes 491528 | tf_op jit(solution)/shard_map/ppermute | solution.py:17
  67.6 3.8 %collective-permute-done.6 = f32[2,16,4,320]{3,1,2,0:T(8,128)S(1)} collective-permute-done((f32[2,16,4,320]{3,1,2,0:T(8,128)S(1)}, f32[2,16,4,320]{3,1,2,0:T(8,128)S(1)}, u32[]{:S(2)}, u32[]{:S(2)}) %collective-permute-start.6) | collective-permute-done | bytes 163872 | tf_op jit(solution)/shard_map/ppermute | solution.py:14
  73.1 3.4 %collective-permute-start.9 = (f32[2,4,8,320]{3,2,1,0:T(8,128)S(1)}, f32[2,4,8,320]{3,2,1,0:T(8,128)S(1)}, u32[]{:S(2)}, u32[]{:S(2)}) collective-permute-start(f32[2,4,8,320]{3,2,1,0:T(8,128)S(1)} %get-tuple-element.247), channel_id=1, source_target_pairs={{4,0},{8,4},{12,8},{5,1},{9,5},{13,9},{6,2},{10,6},{14,10},{7,3},{... | collective-permute-start | bytes 245768 | tf_op jit(solution)/shard_map/ppermute | solution.py:17
  76.4 2.5 collective-permute-start.8
  79.6 3.4 %collective-permute-done.8 = f32[2,4,8,320]{3,2,1,0:T(8,128)S(1)} collective-permute-done((f32[2,4,8,320]{3,2,1,0:T(8,128)S(1)}, f32[2,4,8,320]{3,2,1,0:T(8,128)S(1)}, u32[]{:S(2)}, u32[]{:S(2)}) %collective-permute-start.8) | collective-permute-done | bytes 81952 | tf_op jit(solution)/shard_map/ppermute | solution.py:14
  85.0 2.4 collective-permute-start.10
  88.2 3.8 %collective-permute-done.10 = f32[2,16,4,320]{3,1,2,0:T(8,128)S(1)} collective-permute-done((f32[2,16,4,320]{3,1,2,0:T(8,128)S(1)}, f32[2,16,4,320]{3,1,2,0:T(8,128)S(1)}, u32[]{:S(2)}, u32[]{:S(2)}) %collective-permute-start.10) | collective-permute-done | bytes 163872 | tf_op jit(solution)/shard_map/ppermute | solution.py:14
  95.7 3.9 %collective-permute-start.12 = (f32[2,4,8,320]{3,2,1,0:T(8,128)S(1)}, f32[2,4,8,320]{3,2,1,0:T(8,128)S(1)}, u32[]{:S(2)}, u32[]{:S(2)}) collective-permute-start(f32[2,4,8,320]{3,2,1,0:T(8,128)S(1)} %get-tuple-element.244), channel_id=1, source_target_pairs={{0,4},{4,8},{8,12},{1,5},{5,9},{9,13},{2,6},{6,10},{10,14},{3,7},{... | collective-permute-start | bytes 245768 | tf_op jit(solution)/shard_map/ppermute | solution.py:14
  107.5 3.8 %collective-permute-done.14 = f32[2,16,4,320]{3,1,2,0:T(8,128)S(1)} collective-permute-done((f32[2,16,4,320]{3,1,2,0:T(8,128)S(1)}, f32[2,16,4,320]{3,1,2,0:T(8,128)S(1)}, u32[]{:S(2)}, u32[]{:S(2)}) %collective-permute-start.14) | collective-permute-done | bytes 163872 | tf_op jit(solution)/shard_map/ppermute | solution.py:14
  114.9 3.9 %collective-permute-start.16 = (f32[2,4,8,320]{3,2,1,0:T(8,128)S(1)}, f32[2,4,8,320]{3,2,1,0:T(8,128)S(1)}, u32[]{:S(2)}, u32[]{:S(2)}) collective-permute-start(f32[2,4,8,320]{3,2,1,0:T(8,128)S(1)} %get-tuple-element.242), channel_id=1, source_target_pairs={{0,4},{4,8},{8,12},{1,5},{5,9},{9,13},{2,6},{6,10},{10,14},{3,7},{... | collective-permute-start | bytes 245768 | tf_op jit(solution)/shard_map/ppermute | solution.py:14
  126.7 3.8 %collective-permute-done.18 = f32[2,16,4,320]{3,1,2,0:T(8,128)S(1)} collective-permute-done((f32[2,16,4,320]{3,1,2,0:T(8,128)S(1)}, f32[2,16,4,320]{3,1,2,0:T(8,128)S(1)}, u32[]{:S(2)}, u32[]{:S(2)}) %collective-permute-start.18) | collective-permute-done | bytes 163872 | tf_op jit(solution)/shard_map/ppermute | solution.py:14
  134.2 3.9 %collective-permute-start.20 = (f32[2,4,8,320]{3,2,1,0:T(8,128)S(1)}, f32[2,4,8,320]{3,2,1,0:T(8,128)S(1)}, u32[]{:S(2)}, u32[]{:S(2)}) collective-permute-start(f32[2,4,8,320]{3,2,1,0:T(8,128)S(1)} %get-tuple-element.240), channel_id=1, source_target_pairs={{0,4},{4,8},{8,12},{1,5},{5,9},{9,13},{2,6},{6,10},{10,14},{3,7},{... | collective-permute-start | bytes 245768 | tf_op jit(solution)/shard_map/ppermute | solution.py:14
  142.7 2.6 %collective-permute-start.22 = (f32[2,16,4,320]{3,1,2,0:T(8,128)S(1)}, f32[2,16,4,320]{3,1,2,0:T(8,128)S(1)}, u32[]{:S(2)}, u32[]{:S(2)}) collective-permute-start(f32[2,16,4,320]{3,1,2,0:T(8,128)S(1)} %copy.738), channel_id=1, source_target_pairs={{0,1},{1,2},{2,3},{4,5},{5,6},{6,7},{8,9},{9,10},{10,11},{12,13},{... | collective-permute-start | bytes 491528 | tf_op jit(solution)/shard_map/ppermute | solution.py:14
  146.0 3.8 %collective-permute-done.22 = f32[2,16,4,320]{3,1,2,0:T(8,128)S(1)} collective-permute-done((f32[2,16,4,320]{3,1,2,0:T(8,128)S(1)}, f32[2,16,4,320]{3,1,2,0:T(8,128)S(1)}, u32[]{:S(2)}, u32[]{:S(2)}) %collective-permute-start.22) | collective-permute-done | bytes 163872 | tf_op jit(solution)/shard_map/ppermute | solution.py:14
  153.4 3.9 %collective-permute-start.24 = (f32[2,4,8,320]{3,2,1,0:T(8,128)S(1)}, f32[2,4,8,320]{3,2,1,0:T(8,128)S(1)}, u32[]{:S(2)}, u32[]{:S(2)}) collective-permute-start(f32[2,4,8,320]{3,2,1,0:T(8,128)S(1)} %get-tuple-element.238), channel_id=1, source_target_pairs={{0,4},{4,8},{8,12},{1,5},{5,9},{9,13},{2,6},{6,10},{10,14},{3,7},{... | collective-permute-start | bytes 245768 | tf_op jit(solution)/shard_map/ppermute | solution.py:14
  165.2 3.8 %collective-permute-done.26 = f32[2,16,4,320]{3,1,2,0:T(8,128)S(1)} collective-permute-done((f32[2,16,4,320]{3,1,2,0:T(8,128)S(1)}, f32[2,16,4,320]{3,1,2,0:T(8,128)S(1)}, u32[]{:S(2)}, u32[]{:S(2)}) %collective-permute-start.26) | collective-permute-done | bytes 163872 | tf_op jit(solution)/shard_map/ppermute | solution.py:14
  172.7 3.9 %collective-permute-start.28 = (f32[2,4,8,320]{3,2,1,0:T(8,128)S(1)}, f32[2,4,8,320]{3,2,1,0:T(8,128)S(1)}, u32[]{:S(2)}, u32[]{:S(2)}) collective-permute-start(f32[2,4,8,320]{3,2,1,0:T(8,128)S(1)} %get-tuple-element.236), channel_id=1, source_target_pairs={{0,4},{4,8},{8,12},{1,5},{5,9},{9,13},{2,6},{6,10},{10,14},{3,7},{... | collective-permute-start | bytes 245768 | tf_op jit(solution)/shard_map/ppermute | solution.py:14
  184.5 3.8 %collective-permute-done.30 = f32[2,16,4,320]{3,1,2,0:T(8,128)S(1)} collective-permute-done((f32[2,16,4,320]{3,1,2,0:T(8,128)S(1)}, f32[2,16,4,320]{3,1,2,0:T(8,128)S(1)}, u32[]{:S(2)}, u32[]{:S(2)}) %collective-permute-start.30) | collective-permute-done | bytes 163872 | tf_op jit(solution)/shard_map/ppermute | solution.py:14
  191.9 3.9 %collective-permute-start.32 = (f32[2,4,8,320]{3,2,1,0:T(8,128)S(1)}, f32[2,4,8,320]{3,2,1,0:T(8,128)S(1)}, u32[]{:S(2)}, u32[]{:S(2)}) collective-permute-start(f32[2,4,8,320]{3,2,1,0:T(8,128)S(1)} %get-tuple-element.234), channel_id=1, source_target_pairs={{0,4},{4,8},{8,12},{1,5},{5,9},{9,13},{2,6},{6,10},{10,14},{3,7},{... | collective-permute-start | bytes 245768 | tf_op jit(solution)/shard_map/ppermute | solution.py:14
  203.8 3.8 %collective-permute-done.34 = f32[2,16,4,320]{3,1,2,0:T(8,128)S(1)} collective-permute-done((f32[2,16,4,320]{3,1,2,0:T(8,128)S(1)}, f32[2,16,4,320]{3,1,2,0:T(8,128)S(1)}, u32[]{:S(2)}, u32[]{:S(2)}) %collective-permute-start.34) | collective-permute-done | bytes 163872 | tf_op jit(solution)/shard_map/ppermute | solution.py:14
  211.4 3.9 %collective-permute-start.36 = (f32[2,4,8,320]{3,2,1,0:T(8,128)S(1)}, f32[2,4,8,320]{3,2,1,0:T(8,128)S(1)}, u32[]{:S(2)}, u32[]{:S(2)}) collective-permute-start(f32[2,4,8,320]{3,2,1,0:T(8,128)S(1)} %get-tuple-element.232), channel_id=1, source_target_pairs={{0,4},{4,8},{8,12},{1,5},{5,9},{9,13},{2,6},{6,10},{10,14},{3,7},{... | collective-permute-start | bytes 245768 | tf_op jit(solution)/shard_map/ppermute | solution.py:14
  240.4 3.7 %collective-permute-done.38 = f32[2,16,4,320]{3,1,2,0:T(8,128)S(1)} collective-permute-done((f32[2,16,4,320]{3,1,2,0:T(8,128)S(1)}, f32[2,16,4,320]{3,1,2,0:T(8,128)S(1)}, u32[]{:S(2)}, u32[]{:S(2)}) %collective-permute-start.38) | collective-permute-done | bytes 163872 | tf_op jit(solution)/shard_map/ppermute | solution.py:14
  247.3 7.1 %fusion.361 = (f32[8,8,320]{2,1,0:T(8,128)}, f32[8,8,320]{2,1,0:T(8,128)}) fusion(f32[8,8,320]{2,1,0:T(8,128)S(1)} %multiply_add_fusion.1, f32[8,8,320]{2,1,0:T(8,128)S(1)} %multiply_add_fusion.3, f32[8,8,320]{2,1,0:T(8,128)S(1)} %multiply_add_fusion.4, f32[8,8,320]{2,1,0:T(8,128)S(1)} %multiply_add_fusion.8, f32[8,8,320]{2,1,0:T(8,128)S(1)} %copy-done.7, ...), kind=kLoop, calls=%fused_computation.864 | loop fusion | flops 1228800 | bytes 1556530 | tf_op jit(solution)/shard_map/add | solution.py:116
  (231 shorter events, 96.8 us)
Async XLA Ops:
  1.6 17.6 %collective-permute-start.1 = (f32[2,4,8,320]{3,2,1,0:T(8,128)S(1)}, f32[2,4,8,320]{3,2,1,0:T(8,128)S(1)}, u32[]{:S(2)}, u32[]{:S(2)}) collective-permute-start(f32[2,4,8,320]{3,2,1,0:T(8,128)S(1)} %get-tuple-element.251), channel_id=1, source_target_pairs={{4,0},{8,4},{12,8},{5,1},{9,5},{13,9},{6,2},{10,6},{14,10},{7,3},{... | collective-permute-start | bytes 245768 | tf_op jit(solution)/shard_map/ppermute | solution.py:17
  4.1 15.1 %collective-permute-start = (f32[2,4,8,320]{3,2,1,0:T(8,128)S(1)}, f32[2,4,8,320]{3,2,1,0:T(8,128)S(1)}, u32[]{:S(2)}, u32[]{:S(2)}) collective-permute-start(f32[2,4,8,320]{3,2,1,0:T(8,128)S(1)} %get-tuple-element.250), channel_id=1, source_target_pairs={{0,4},{4,8},{8,12},{1,5},{5,9},{9,13},{2,6},{6,10},{10,14},{3,7},{... | collective-permute-start | bytes 245768 | tf_op jit(solution)/shard_map/ppermute | solution.py:14
  19.3 26.6 %collective-permute-start.3 = (f32[2,16,4,320]{3,1,2,0:T(8,128)S(1)}, f32[2,16,4,320]{3,1,2,0:T(8,128)S(1)}, u32[]{:S(2)}, u32[]{:S(2)}) collective-permute-start(f32[2,16,4,320]{3,1,2,0:T(8,128)S(1)} %copy.729), channel_id=1, source_target_pairs={{1,0},{2,1},{3,2},{5,4},{6,5},{7,6},{9,8},{10,9},{11,10},{13,12},{... | collective-permute-start | bytes 491528 | tf_op jit(solution)/shard_map/ppermute | solution.py:17
  21.3 24.7 %collective-permute-start.2 = (f32[2,16,4,320]{3,1,2,0:T(8,128)S(1)}, f32[2,16,4,320]{3,1,2,0:T(8,128)S(1)}, u32[]{:S(2)}, u32[]{:S(2)}) collective-permute-start(f32[2,16,4,320]{3,1,2,0:T(8,128)S(1)} %copy.728), channel_id=1, source_target_pairs={{0,1},{1,2},{2,3},{4,5},{5,6},{6,7},{8,9},{9,10},{10,11},{12,13},{... | collective-permute-start | bytes 491528 | tf_op jit(solution)/shard_map/ppermute | solution.py:14
  49.3 6.9 %collective-permute-start.5 = (f32[2,4,8,320]{3,2,1,0:T(8,128)S(1)}, f32[2,4,8,320]{3,2,1,0:T(8,128)S(1)}, u32[]{:S(2)}, u32[]{:S(2)}) collective-permute-start(f32[2,4,8,320]{3,2,1,0:T(8,128)S(1)} %get-tuple-element.249), channel_id=1, source_target_pairs={{4,0},{8,4},{12,8},{5,1},{9,5},{13,9},{6,2},{10,6},{14,10},{7,3},{... | collective-permute-start | bytes 245768 | tf_op jit(solution)/shard_map/ppermute | solution.py:17
  52.6 8.0 %collective-permute-start.4 = (f32[2,4,8,320]{3,2,1,0:T(8,128)S(1)}, f32[2,4,8,320]{3,2,1,0:T(8,128)S(1)}, u32[]{:S(2)}, u32[]{:S(2)}) collective-permute-start(f32[2,4,8,320]{3,2,1,0:T(8,128)S(1)} %get-tuple-element.248), channel_id=1, source_target_pairs={{0,4},{4,8},{8,12},{1,5},{5,9},{9,13},{2,6},{6,10},{10,14},{3,7},{... | collective-permute-start | bytes 245768 | tf_op jit(solution)/shard_map/ppermute | solution.py:14
  60.7 6.8 %collective-permute-start.7 = (f32[2,16,4,320]{3,1,2,0:T(8,128)S(1)}, f32[2,16,4,320]{3,1,2,0:T(8,128)S(1)}, u32[]{:S(2)}, u32[]{:S(2)}) collective-permute-start(f32[2,16,4,320]{3,1,2,0:T(8,128)S(1)} %copy.731), channel_id=1, source_target_pairs={{1,0},{2,1},{3,2},{5,4},{6,5},{7,6},{9,8},{10,9},{11,10},{13,12},{... | collective-permute-start | bytes 491528 | tf_op jit(solution)/shard_map/ppermute | solution.py:17
  64.4 7.0 %collective-permute-start.6 = (f32[2,16,4,320]{3,1,2,0:T(8,128)S(1)}, f32[2,16,4,320]{3,1,2,0:T(8,128)S(1)}, u32[]{:S(2)}, u32[]{:S(2)}) collective-permute-start(f32[2,16,4,320]{3,1,2,0:T(8,128)S(1)} %copy.730), channel_id=1, source_target_pairs={{0,1},{1,2},{2,3},{4,5},{5,6},{6,7},{8,9},{9,10},{10,11},{12,13},{... | collective-permute-start | bytes 491528 | tf_op jit(solution)/shard_map/ppermute | solution.py:14
  73.1 6.5 %collective-permute-start.9 = (f32[2,4,8,320]{3,2,1,0:T(8,128)S(1)}, f32[2,4,8,320]{3,2,1,0:T(8,128)S(1)}, u32[]{:S(2)}, u32[]{:S(2)}) collective-permute-start(f32[2,4,8,320]{3,2,1,0:T(8,128)S(1)} %get-tuple-element.247), channel_id=1, source_target_pairs={{4,0},{8,4},{12,8},{5,1},{9,5},{13,9},{6,2},{10,6},{14,10},{7,3},{... | collective-permute-start | bytes 245768 | tf_op jit(solution)/shard_map/ppermute | solution.py:17
  76.4 6.5 %collective-permute-start.8 = (f32[2,4,8,320]{3,2,1,0:T(8,128)S(1)}, f32[2,4,8,320]{3,2,1,0:T(8,128)S(1)}, u32[]{:S(2)}, u32[]{:S(2)}) collective-permute-start(f32[2,4,8,320]{3,2,1,0:T(8,128)S(1)} %get-tuple-element.246), channel_id=1, source_target_pairs={{0,4},{4,8},{8,12},{1,5},{5,9},{9,13},{2,6},{6,10},{10,14},{3,7},{... | collective-permute-start | bytes 245768 | tf_op jit(solution)/shard_map/ppermute | solution.py:14
  85.0 7.0 %collective-permute-start.10 = (f32[2,16,4,320]{3,1,2,0:T(8,128)S(1)}, f32[2,16,4,320]{3,1,2,0:T(8,128)S(1)}, u32[]{:S(2)}, u32[]{:S(2)}) collective-permute-start(f32[2,16,4,320]{3,1,2,0:T(8,128)S(1)} %copy.732), channel_id=1, source_target_pairs={{0,1},{1,2},{2,3},{4,5},{5,6},{6,7},{8,9},{9,10},{10,11},{12,13},{... | collective-permute-start | bytes 491528 | tf_op jit(solution)/shard_map/ppermute | solution.py:14
  93.7 6.5 %collective-permute-start.13 = (f32[2,4,8,320]{3,2,1,0:T(8,128)S(1)}, f32[2,4,8,320]{3,2,1,0:T(8,128)S(1)}, u32[]{:S(2)}, u32[]{:S(2)}) collective-permute-start(f32[2,4,8,320]{3,2,1,0:T(8,128)S(1)} %get-tuple-element.245), channel_id=1, source_target_pairs={{4,0},{8,4},{12,8},{5,1},{9,5},{13,9},{6,2},{10,6},{14,10},{7,3},{... | collective-permute-start | bytes 245768 | tf_op jit(solution)/shard_map/ppermute | solution.py:17
  95.7 6.5 %collective-permute-start.12 = (f32[2,4,8,320]{3,2,1,0:T(8,128)S(1)}, f32[2,4,8,320]{3,2,1,0:T(8,128)S(1)}, u32[]{:S(2)}, u32[]{:S(2)}) collective-permute-start(f32[2,4,8,320]{3,2,1,0:T(8,128)S(1)} %get-tuple-element.244), channel_id=1, source_target_pairs={{0,4},{4,8},{8,12},{1,5},{5,9},{9,13},{2,6},{6,10},{10,14},{3,7},{... | collective-permute-start | bytes 245768 | tf_op jit(solution)/shard_map/ppermute | solution.py:14
  104.2 7.0 %collective-permute-start.14 = (f32[2,16,4,320]{3,1,2,0:T(8,128)S(1)}, f32[2,16,4,320]{3,1,2,0:T(8,128)S(1)}, u32[]{:S(2)}, u32[]{:S(2)}) collective-permute-start(f32[2,16,4,320]{3,1,2,0:T(8,128)S(1)} %copy.734), channel_id=1, source_target_pairs={{0,1},{1,2},{2,3},{4,5},{5,6},{6,7},{8,9},{9,10},{10,11},{12,13},{... | collective-permute-start | bytes 491528 | tf_op jit(solution)/shard_map/ppermute | solution.py:14
  113.0 6.5 %collective-permute-start.17 = (f32[2,4,8,320]{3,2,1,0:T(8,128)S(1)}, f32[2,4,8,320]{3,2,1,0:T(8,128)S(1)}, u32[]{:S(2)}, u32[]{:S(2)}) collective-permute-start(f32[2,4,8,320]{3,2,1,0:T(8,128)S(1)} %get-tuple-element.243), channel_id=1, source_target_pairs={{4,0},{8,4},{12,8},{5,1},{9,5},{13,9},{6,2},{10,6},{14,10},{7,3},{... | collective-permute-start | bytes 245768 | tf_op jit(solution)/shard_map/ppermute | solution.py:17
  114.9 6.5 %collective-permute-start.16 = (f32[2,4,8,320]{3,2,1,0:T(8,128)S(1)}, f32[2,4,8,320]{3,2,1,0:T(8,128)S(1)}, u32[]{:S(2)}, u32[]{:S(2)}) collective-permute-start(f32[2,4,8,320]{3,2,1,0:T(8,128)S(1)} %get-tuple-element.242), channel_id=1, source_target_pairs={{0,4},{4,8},{8,12},{1,5},{5,9},{9,13},{2,6},{6,10},{10,14},{3,7},{... | collective-permute-start | bytes 245768 | tf_op jit(solution)/shard_map/ppermute | solution.py:14
  123.5 7.0 %collective-permute-start.18 = (f32[2,16,4,320]{3,1,2,0:T(8,128)S(1)}, f32[2,16,4,320]{3,1,2,0:T(8,128)S(1)}, u32[]{:S(2)}, u32[]{:S(2)}) collective-permute-start(f32[2,16,4,320]{3,1,2,0:T(8,128)S(1)} %copy.736), channel_id=1, source_target_pairs={{0,1},{1,2},{2,3},{4,5},{5,6},{6,7},{8,9},{9,10},{10,11},{12,13},{... | collective-permute-start | bytes 491528 | tf_op jit(solution)/shard_map/ppermute | solution.py:14
  132.2 6.5 %collective-permute-start.21 = (f32[2,4,8,320]{3,2,1,0:T(8,128)S(1)}, f32[2,4,8,320]{3,2,1,0:T(8,128)S(1)}, u32[]{:S(2)}, u32[]{:S(2)}) collective-permute-start(f32[2,4,8,320]{3,2,1,0:T(8,128)S(1)} %get-tuple-element.241), channel_id=1, source_target_pairs={{4,0},{8,4},{12,8},{5,1},{9,5},{13,9},{6,2},{10,6},{14,10},{7,3},{... | collective-permute-start | bytes 245768 | tf_op jit(solution)/shard_map/ppermute | solution.py:17
  134.2 6.5 %collective-permute-start.20 = (f32[2,4,8,320]{3,2,1,0:T(8,128)S(1)}, f32[2,4,8,320]{3,2,1,0:T(8,128)S(1)}, u32[]{:S(2)}, u32[]{:S(2)}) collective-permute-start(f32[2,4,8,320]{3,2,1,0:T(8,128)S(1)} %get-tuple-element.240), channel_id=1, source_target_pairs={{0,4},{4,8},{8,12},{1,5},{5,9},{9,13},{2,6},{6,10},{10,14},{3,7},{... | collective-permute-start | bytes 245768 | tf_op jit(solution)/shard_map/ppermute | solution.py:14
  142.7 7.0 %collective-permute-start.22 = (f32[2,16,4,320]{3,1,2,0:T(8,128)S(1)}, f32[2,16,4,320]{3,1,2,0:T(8,128)S(1)}, u32[]{:S(2)}, u32[]{:S(2)}) collective-permute-start(f32[2,16,4,320]{3,1,2,0:T(8,128)S(1)} %copy.738), channel_id=1, source_target_pairs={{0,1},{1,2},{2,3},{4,5},{5,6},{6,7},{8,9},{9,10},{10,11},{12,13},{... | collective-permute-start | bytes 491528 | tf_op jit(solution)/shard_map/ppermute | solution.py:14
  151.5 6.5 %collective-permute-start.25 = (f32[2,4,8,320]{3,2,1,0:T(8,128)S(1)}, f32[2,4,8,320]{3,2,1,0:T(8,128)S(1)}, u32[]{:S(2)}, u32[]{:S(2)}) collective-permute-start(f32[2,4,8,320]{3,2,1,0:T(8,128)S(1)} %get-tuple-element.239), channel_id=1, source_target_pairs={{4,0},{8,4},{12,8},{5,1},{9,5},{13,9},{6,2},{10,6},{14,10},{7,3},{... | collective-permute-start | bytes 245768 | tf_op jit(solution)/shard_map/ppermute | solution.py:17
  153.4 6.5 %collective-permute-start.24 = (f32[2,4,8,320]{3,2,1,0:T(8,128)S(1)}, f32[2,4,8,320]{3,2,1,0:T(8,128)S(1)}, u32[]{:S(2)}, u32[]{:S(2)}) collective-permute-start(f32[2,4,8,320]{3,2,1,0:T(8,128)S(1)} %get-tuple-element.238), channel_id=1, source_target_pairs={{0,4},{4,8},{8,12},{1,5},{5,9},{9,13},{2,6},{6,10},{10,14},{3,7},{... | collective-permute-start | bytes 245768 | tf_op jit(solution)/shard_map/ppermute | solution.py:14
  162.0 7.0 %collective-permute-start.26 = (f32[2,16,4,320]{3,1,2,0:T(8,128)S(1)}, f32[2,16,4,320]{3,1,2,0:T(8,128)S(1)}, u32[]{:S(2)}, u32[]{:S(2)}) collective-permute-start(f32[2,16,4,320]{3,1,2,0:T(8,128)S(1)} %copy.740), channel_id=1, source_target_pairs={{0,1},{1,2},{2,3},{4,5},{5,6},{6,7},{8,9},{9,10},{10,11},{12,13},{... | collective-permute-start | bytes 491528 | tf_op jit(solution)/shard_map/ppermute | solution.py:14
  170.8 6.5 %collective-permute-start.29 = (f32[2,4,8,320]{3,2,1,0:T(8,128)S(1)}, f32[2,4,8,320]{3,2,1,0:T(8,128)S(1)}, u32[]{:S(2)}, u32[]{:S(2)}) collective-permute-start(f32[2,4,8,320]{3,2,1,0:T(8,128)S(1)} %get-tuple-element.237), channel_id=1, source_target_pairs={{4,0},{8,4},{12,8},{5,1},{9,5},{13,9},{6,2},{10,6},{14,10},{7,3},{... | collective-permute-start | bytes 245768 | tf_op jit(solution)/shard_map/ppermute | solution.py:17
  172.7 6.5 %collective-permute-start.28 = (f32[2,4,8,320]{3,2,1,0:T(8,128)S(1)}, f32[2,4,8,320]{3,2,1,0:T(8,128)S(1)}, u32[]{:S(2)}, u32[]{:S(2)}) collective-permute-start(f32[2,4,8,320]{3,2,1,0:T(8,128)S(1)} %get-tuple-element.236), channel_id=1, source_target_pairs={{0,4},{4,8},{8,12},{1,5},{5,9},{9,13},{2,6},{6,10},{10,14},{3,7},{... | collective-permute-start | bytes 245768 | tf_op jit(solution)/shard_map/ppermute | solution.py:14
  181.3 7.0 %collective-permute-start.30 = (f32[2,16,4,320]{3,1,2,0:T(8,128)S(1)}, f32[2,16,4,320]{3,1,2,0:T(8,128)S(1)}, u32[]{:S(2)}, u32[]{:S(2)}) collective-permute-start(f32[2,16,4,320]{3,1,2,0:T(8,128)S(1)} %copy.742), channel_id=1, source_target_pairs={{0,1},{1,2},{2,3},{4,5},{5,6},{6,7},{8,9},{9,10},{10,11},{12,13},{... | collective-permute-start | bytes 491528 | tf_op jit(solution)/shard_map/ppermute | solution.py:14
  190.0 6.5 %collective-permute-start.33 = (f32[2,4,8,320]{3,2,1,0:T(8,128)S(1)}, f32[2,4,8,320]{3,2,1,0:T(8,128)S(1)}, u32[]{:S(2)}, u32[]{:S(2)}) collective-permute-start(f32[2,4,8,320]{3,2,1,0:T(8,128)S(1)} %get-tuple-element.235), channel_id=1, source_target_pairs={{4,0},{8,4},{12,8},{5,1},{9,5},{13,9},{6,2},{10,6},{14,10},{7,3},{... | collective-permute-start | bytes 245768 | tf_op jit(solution)/shard_map/ppermute | solution.py:17
  191.9 6.5 %collective-permute-start.32 = (f32[2,4,8,320]{3,2,1,0:T(8,128)S(1)}, f32[2,4,8,320]{3,2,1,0:T(8,128)S(1)}, u32[]{:S(2)}, u32[]{:S(2)}) collective-permute-start(f32[2,4,8,320]{3,2,1,0:T(8,128)S(1)} %get-tuple-element.234), channel_id=1, source_target_pairs={{0,4},{4,8},{8,12},{1,5},{5,9},{9,13},{2,6},{6,10},{10,14},{3,7},{... | collective-permute-start | bytes 245768 | tf_op jit(solution)/shard_map/ppermute | solution.py:14
  200.5 7.0 %collective-permute-start.34 = (f32[2,16,4,320]{3,1,2,0:T(8,128)S(1)}, f32[2,16,4,320]{3,1,2,0:T(8,128)S(1)}, u32[]{:S(2)}, u32[]{:S(2)}) collective-permute-start(f32[2,16,4,320]{3,1,2,0:T(8,128)S(1)} %copy.744), channel_id=1, source_target_pairs={{0,1},{1,2},{2,3},{4,5},{5,6},{6,7},{8,9},{9,10},{10,11},{12,13},{... | collective-permute-start | bytes 491528 | tf_op jit(solution)/shard_map/ppermute | solution.py:14
  209.3 25.6 %collective-permute-start.37 = (f32[2,4,8,320]{3,2,1,0:T(8,128)S(1)}, f32[2,4,8,320]{3,2,1,0:T(8,128)S(1)}, u32[]{:S(2)}, u32[]{:S(2)}) collective-permute-start(f32[2,4,8,320]{3,2,1,0:T(8,128)S(1)} %get-tuple-element.233), channel_id=1, source_target_pairs={{4,0},{8,4},{12,8},{5,1},{9,5},{13,9},{6,2},{10,6},{14,10},{7,3},{... | collective-permute-start | bytes 245768 | tf_op jit(solution)/shard_map/ppermute | solution.py:17
  211.4 23.6 %collective-permute-start.36 = (f32[2,4,8,320]{3,2,1,0:T(8,128)S(1)}, f32[2,4,8,320]{3,2,1,0:T(8,128)S(1)}, u32[]{:S(2)}, u32[]{:S(2)}) collective-permute-start(f32[2,4,8,320]{3,2,1,0:T(8,128)S(1)} %get-tuple-element.232), channel_id=1, source_target_pairs={{0,4},{4,8},{8,12},{1,5},{5,9},{9,13},{2,6},{6,10},{10,14},{3,7},{... | collective-permute-start | bytes 245768 | tf_op jit(solution)/shard_map/ppermute | solution.py:14
  237.1 7.0 %collective-permute-start.38 = (f32[2,16,4,320]{3,1,2,0:T(8,128)S(1)}, f32[2,16,4,320]{3,1,2,0:T(8,128)S(1)}, u32[]{:S(2)}, u32[]{:S(2)}) collective-permute-start(f32[2,16,4,320]{3,1,2,0:T(8,128)S(1)} %copy.746), channel_id=1, source_target_pairs={{0,1},{1,2},{2,3},{4,5},{5,6},{6,7},{8,9},{9,10},{10,11},{12,13},{... | collective-permute-start | bytes 491528 | tf_op jit(solution)/shard_map/ppermute | solution.py:14
  (22 other events, 187.4 us)
where the time goes:
time: 256 us; the launch traced here: 254 us
  starting transfers between devices  103 us (40%)
  waiting for transfers between devices  64.8 us (25%)
  other arithmetic  32.2 us (13%)
  blocking collectives  24.6 us (10%)
  between operations  22.2 us (9%)
  local copies, waits for them, and re-layouts  7.13 us (3%)
    ppermute x20, starting transfers between devices, with_halo(): lax.ppermute(lax.slice_in_dim(block, block.shape[dim] - width, None, axis...  59.8 us
    ppermute x20, waiting for transfers between devices, with_halo(): lax.ppermute(lax.slice_in_dim(block, block.shape[dim] - width, None, axis...  53 us
    ppermute x20, starting transfers between devices, with_halo(): lax.ppermute(lax.slice_in_dim(block, 0, width, axis=dim), axis, backward)  43.6 us
    all_gather x1, blocking collectives, body(): values = lax.all_gather(traces, ('gx', 'gy'), axis=1, tiled=True)  15.2 us
    ppermute x20, waiting for transfers between devices, with_halo(): lax.ppermute(lax.slice_in_dim(block, 0, width, axis=dim), axis, backward)  11.7 us
    convert_element_type x10, other arithmetic, body(): source_field.astype(jnp.bfloat16)[None]  9.89 us
    unnamed x1, blocking collectives  9.37 us
    add x1, other arithmetic, body(): imaged = imaged + jnp.where(present, snapshot * receiver_field, 0.0)  7.05 us
  transfers between devices with their start and end apart: 40, of which 33 were waited for; matrix products, arithmetic and copies ran while one was open for 4% of the time, Pallas kernels for 0%

commit v1 on v0

--- a/solution.py
+++ b/solution.py
@@ -65,7 +65,10 @@
     span_x = block_x + 2 * border
     span_y = block_y + 2 * border
     plane_cells = span_x * span_y
-    values = lax.all_gather(traces, ("gx", "gy"), axis=1, tiled=True)
+    count_2 = lax.axis_size(("gx", "gy"))
+    blocks = jnp.stack([traces for _ in range(count_2)])
+    blocks = lax.all_to_all(blocks, ("gx", "gy"), split_axis=0, concat_axis=0)
+    values = jnp.concatenate(blocks, axis=1)
     cell_ids = lax.all_gather(receiver_cells, ("gx", "gy"), axis=1, tiled=True)
     cell_ids = cell_ids[0]
     local_x = cell_ids // grid_y - (start_x - border)

time: 256 us -> 246 us (0.961)
  blocking collectives: 24.6 us -> 9.48 us
  starting transfers between devices: 103 us -> 107 us
    all_gather x1 -> x0, blocking collectives: 15.2 us -> none  [body(): values = lax.all_gather(traces, ('gx', 'gy'), axis=1, tiled=True)]
    all_to_all x0 -> x1, starting transfers between devices: none -> 5.25 us  [body(): blocks = lax.all_to_all(blocks, ('gx', 'gy'), split_axis=0, concat_axis=0)]
  transfers between devices with their start and end apart: 40 -> 41, of which waited for: 33 -> 33; matrix products, arithmetic and copies ran while one was open for 4% -> 5% of each run, Pallas kernels for 0% -> 0%
where the time goes in v1:
time: 246 us; the launch traced here: 244 us
  starting transfers between devices  107 us (43%)
  waiting for transfers between devices  63.4 us (26%)
  other arithmetic  32.9 us (13%)
  between operations  22.1 us (9%)
  blocking collectives  9.48 us (4%)
  local copies, waits for them, and re-layouts  8.56 us (3%)
    ppermute x20, starting transfers between devices, with_halo(): lax.ppermute(lax.slice_in_dim(block, block.shape[dim] - width, None, axis...  59.8 us
    ppermute x20, waiting for transfers between devices, with_halo(): lax.ppermute(lax.slice_in_dim(block, block.shape[dim] - width, None, axis...  52.2 us
    ppermute x20, starting transfers between devices, with_halo(): lax.ppermute(lax.slice_in_dim(block, 0, width, axis=dim), axis, backward)  42.3 us
    ppermute x20, waiting for transfers between devices, with_halo(): lax.ppermute(lax.slice_in_dim(block, 0, width, axis=dim), axis, backward)  11.1 us
    convert_element_type x10, other arithmetic, body(): source_field.astype(jnp.bfloat16)[None]  9.81 us
    unnamed x1, blocking collectives  9.48 us
    add x1, other arithmetic, body(): imaged = imaged + jnp.where(present, snapshot * receiver_field, 0.0)  7.04 us
    scatter-add x1, other arithmetic, body(): injected = jnp.zeros((total_steps, plane_cells), jnp.float32).at[:, local...  6.04 us
  transfers between devices with their start and end apart: 41, of which 33 were waited for; matrix products, arithmetic and copies ran while one was open for 5% of the time, Pallas kernels for 0%

profile of v1, /device:TPU:18, one launch (start us, length us, event | category | flops | bytes accessed | tf_op | source)
XLA Modules:
  0.0 243.7 jit_solution(6953681213085616724)
XLA Ops:
  3.9 3.5 %collective-permute-start = (f32[2,4,8,320]{3,2,1,0:T(8,128)S(1)}, f32[2,4,8,320]{3,2,1,0:T(8,128)S(1)}, u32[]{:S(2)}, u32[]{:S(2)}) collective-permute-start(f32[2,4,8,320]{3,2,1,0:T(8,128)S(1)} %get-tuple-element.256), channel_id=1, source_target_pairs={{0,4},{4,8},{8,12},{1,5},{5,9},{9,13},{2,6},{6,10},{10,14},{3,7},{... | collective-permute-start | bytes 245768 | tf_op jit(solution)/shard_map/ppermute | solution.py:14
  8.2 5.2 %all-to-all-start = ((f32[16,1,640]{2,1,0:T(1,128)}), f32[16,1,640]{2,1,0:T(1,128)S(1)}, u32[]{:S(2)}, u32[]{:S(2)}) async-start(f32[16,1,640]{2,1,0:T(1,128)} %reshape.617), calls=%async_computation | async-start | bytes 81920 | tf_op jit(solution)/shard_map/all_to_all | solution.py:70
  15.5 9.5 %all-reduce.20 = s32[1024]{0:T(1024)S(1)} all-reduce(s32[1024]{0:T(1024)S(1)} %bitcast_dynamic-update-slice_fusion), channel_id=1, replica_groups=mesh['shot'=2,'gx'=4,'gy'=4] {'gx','gy'}, use_global_device_ids=true, to_apply=%add.20 | all-reduce | flops 1024 | bytes 8192
  27.3 2.4 collective-permute-start.2
  32.1 6.0 %scatter_custom_fusion = f32[10,64]{0,1:T(8,128)S(1)} fusion(s32[1024]{0:T(1024)S(1)} %bitcast.207, f32[1024,10]{1,0:T(8,128)S(1)} %copy.882, f32[]{:T(128)} %constant.323.clone.1), kind=kCustom, calls=%fused_computation.926 | custom fusion | flops 10240 | bytes 2564 | tf_op jit(solution)/shard_map/scatter-add | solution.py:81
  41.5 3.4 %collective-permute-start.5 = (f32[2,4,8,320]{3,2,1,0:T(8,128)S(1)}, f32[2,4,8,320]{3,2,1,0:T(8,128)S(1)}, u32[]{:S(2)}, u32[]{:S(2)}) collective-permute-start(f32[2,4,8,320]{3,2,1,0:T(8,128)S(1)} %get-tuple-element.255), channel_id=1, source_target_pairs={{4,0},{8,4},{12,8},{5,1},{9,5},{13,9},{6,2},{10,6},{14,10},{7,3},{... | collective-permute-start | bytes 245768 | tf_op jit(solution)/shard_map/ppermute | solution.py:17
  44.9 2.5 %collective-permute-start.4 = (f32[2,4,8,320]{3,2,1,0:T(8,128)S(1)}, f32[2,4,8,320]{3,2,1,0:T(8,128)S(1)}, u32[]{:S(2)}, u32[]{:S(2)}) collective-permute-start(f32[2,4,8,320]{3,2,1,0:T(8,128)S(1)} %get-tuple-element.254), channel_id=1, source_target_pairs={{0,4},{4,8},{8,12},{1,5},{5,9},{9,13},{2,6},{6,10},{10,14},{3,7},{... | collective-permute-start | bytes 245768 | tf_op jit(solution)/shard_map/ppermute | solution.py:14
  48.0 3.4 %collective-permute-done.4 = f32[2,4,8,320]{3,2,1,0:T(8,128)S(1)} collective-permute-done((f32[2,4,8,320]{3,2,1,0:T(8,128)S(1)}, f32[2,4,8,320]{3,2,1,0:T(8,128)S(1)}, u32[]{:S(2)}, u32[]{:S(2)}) %collective-permute-start.4) | collective-permute-done | bytes 81952 | tf_op jit(solution)/shard_map/ppermute | solution.py:14
  57.0 3.8 %collective-permute-done.6 = f32[2,16,4,320]{3,1,2,0:T(8,128)S(1)} collective-permute-done((f32[2,16,4,320]{3,1,2,0:T(8,128)S(1)}, f32[2,16,4,320]{3,1,2,0:T(8,128)S(1)}, u32[]{:S(2)}, u32[]{:S(2)}) %collective-permute-start.6) | collective-permute-done | bytes 163872 | tf_op jit(solution)/shard_map/ppermute | solution.py:14
  62.5 3.5 %collective-permute-start.9 = (f32[2,4,8,320]{3,2,1,0:T(8,128)S(1)}, f32[2,4,8,320]{3,2,1,0:T(8,128)S(1)}, u32[]{:S(2)}, u32[]{:S(2)}) collective-permute-start(f32[2,4,8,320]{3,2,1,0:T(8,128)S(1)} %get-tuple-element.253), channel_id=1, source_target_pairs={{4,0},{8,4},{12,8},{5,1},{9,5},{13,9},{6,2},{10,6},{14,10},{7,3},{... | collective-permute-start | bytes 245768 | tf_op jit(solution)/shard_map/ppermute | solution.py:17
  69.0 3.5 %collective-permute-done.8 = f32[2,4,8,320]{3,2,1,0:T(8,128)S(1)} collective-permute-done((f32[2,4,8,320]{3,2,1,0:T(8,128)S(1)}, f32[2,4,8,320]{3,2,1,0:T(8,128)S(1)}, u32[]{:S(2)}, u32[]{:S(2)}) %collective-permute-start.8) | collective-permute-done | bytes 81952 | tf_op jit(solution)/shard_map/ppermute | solution.py:14
  74.6 2.4 collective-permute-start.10
  77.8 3.8 %collective-permute-done.10 = f32[2,16,4,320]{3,1,2,0:T(8,128)S(1)} collective-permute-done((f32[2,16,4,320]{3,1,2,0:T(8,128)S(1)}, f32[2,16,4,320]{3,1,2,0:T(8,128)S(1)}, u32[]{:S(2)}, u32[]{:S(2)}) %collective-permute-start.10) | collective-permute-done | bytes 163872 | tf_op jit(solution)/shard_map/ppermute | solution.py:14
  85.2 3.9 %collective-permute-start.12 = (f32[2,4,8,320]{3,2,1,0:T(8,128)S(1)}, f32[2,4,8,320]{3,2,1,0:T(8,128)S(1)}, u32[]{:S(2)}, u32[]{:S(2)}) collective-permute-start(f32[2,4,8,320]{3,2,1,0:T(8,128)S(1)} %get-tuple-element.250), channel_id=1, source_target_pairs={{0,4},{4,8},{8,12},{1,5},{5,9},{9,13},{2,6},{6,10},{10,14},{3,7},{... | collective-permute-start | bytes 245768 | tf_op jit(solution)/shard_map/ppermute | solution.py:14
  93.8 2.4 collective-permute-start.14
  97.0 3.8 %collective-permute-done.14 = f32[2,16,4,320]{3,1,2,0:T(8,128)S(1)} collective-permute-done((f32[2,16,4,320]{3,1,2,0:T(8,128)S(1)}, f32[2,16,4,320]{3,1,2,0:T(8,128)S(1)}, u32[]{:S(2)}, u32[]{:S(2)}) %collective-permute-start.14) | collective-permute-done | bytes 163872 | tf_op jit(solution)/shard_map/ppermute | solution.py:14
  104.4 3.9 %collective-permute-start.16 = (f32[2,4,8,320]{3,2,1,0:T(8,128)S(1)}, f32[2,4,8,320]{3,2,1,0:T(8,128)S(1)}, u32[]{:S(2)}, u32[]{:S(2)}) collective-permute-start(f32[2,4,8,320]{3,2,1,0:T(8,128)S(1)} %get-tuple-element.248), channel_id=1, source_target_pairs={{0,4},{4,8},{8,12},{1,5},{5,9},{9,13},{2,6},{6,10},{10,14},{3,7},{... | collective-permute-start | bytes 245768 | tf_op jit(solution)/shard_map/ppermute | solution.py:14
  113.0 2.4 collective-permute-start.18
  116.2 3.8 %collective-permute-done.18 = f32[2,16,4,320]{3,1,2,0:T(8,128)S(1)} collective-permute-done((f32[2,16,4,320]{3,1,2,0:T(8,128)S(1)}, f32[2,16,4,320]{3,1,2,0:T(8,128)S(1)}, u32[]{:S(2)}, u32[]{:S(2)}) %collective-permute-start.18) | collective-permute-done | bytes 163872 | tf_op jit(solution)/shard_map/ppermute | solution.py:14
  123.6 3.9 %collective-permute-start.20 = (f32[2,4,8,320]{3,2,1,0:T(8,128)S(1)}, f32[2,4,8,320]{3,2,1,0:T(8,128)S(1)}, u32[]{:S(2)}, u32[]{:S(2)}) collective-permute-start(f32[2,4,8,320]{3,2,1,0:T(8,128)S(1)} %get-tuple-element.246), channel_id=1, source_target_pairs={{0,4},{4,8},{8,12},{1,5},{5,9},{9,13},{2,6},{6,10},{10,14},{3,7},{... | collective-permute-start | bytes 245768 | tf_op jit(solution)/shard_map/ppermute | solution.py:14
  132.2 2.6 %collective-permute-start.22 = (f32[2,16,4,320]{3,1,2,0:T(8,128)S(1)}, f32[2,16,4,320]{3,1,2,0:T(8,128)S(1)}, u32[]{:S(2)}, u32[]{:S(2)}) collective-permute-start(f32[2,16,4,320]{3,1,2,0:T(8,128)S(1)} %copy.939), channel_id=1, source_target_pairs={{0,1},{1,2},{2,3},{4,5},{5,6},{6,7},{8,9},{9,10},{10,11},{12,13},{... | collective-permute-start | bytes 491528 | tf_op jit(solution)/shard_map/ppermute | solution.py:14
  135.4 3.8 %collective-permute-done.22 = f32[2,16,4,320]{3,1,2,0:T(8,128)S(1)} collective-permute-done((f32[2,16,4,320]{3,1,2,0:T(8,128)S(1)}, f32[2,16,4,320]{3,1,2,0:T(8,128)S(1)}, u32[]{:S(2)}, u32[]{:S(2)}) %collective-permute-start.22) | collective-permute-done | bytes 163872 | tf_op jit(solution)/shard_map/ppermute | solution.py:14
  142.9 3.9 %collective-permute-start.24 = (f32[2,4,8,320]{3,2,1,0:T(8,128)S(1)}, f32[2,4,8,320]{3,2,1,0:T(8,128)S(1)}, u32[]{:S(2)}, u32[]{:S(2)}) collective-permute-start(f32[2,4,8,320]{3,2,1,0:T(8,128)S(1)} %get-tuple-element.244), channel_id=1, source_target_pairs={{0,4},{4,8},{8,12},{1,5},{5,9},{9,13},{2,6},{6,10},{10,14},{3,7},{... | collective-permute-start | bytes 245768 | tf_op jit(solution)/shard_map/ppermute | solution.py:14
  154.7 3.8 %collective-permute-done.26 = f32[2,16,4,320]{3,1,2,0:T(8,128)S(1)} collective-permute-done((f32[2,16,4,320]{3,1,2,0:T(8,128)S(1)}, f32[2,16,4,320]{3,1,2,0:T(8,128)S(1)}, u32[]{:S(2)}, u32[]{:S(2)}) %collective-permute-start.26) | collective-permute-done | bytes 163872 | tf_op jit(solution)/shard_map/ppermute | solution.py:14
  162.2 3.9 %collective-permute-start.28 = (f32[2,4,8,320]{3,2,1,0:T(8,128)S(1)}, f32[2,4,8,320]{3,2,1,0:T(8,128)S(1)}, u32[]{:S(2)}, u32[]{:S(2)}) collective-permute-start(f32[2,4,8,320]{3,2,1,0:T(8,128)S(1)} %get-tuple-element.242), channel_id=1, source_target_pairs={{0,4},{4,8},{8,12},{1,5},{5,9},{9,13},{2,6},{6,10},{10,14},{3,7},{... | collective-permute-start | bytes 245768 | tf_op jit(solution)/shard_map/ppermute | solution.py:14
  174.0 3.8 %collective-permute-done.30 = f32[2,16,4,320]{3,1,2,0:T(8,128)S(1)} collective-permute-done((f32[2,16,4,320]{3,1,2,0:T(8,128)S(1)}, f32[2,16,4,320]{3,1,2,0:T(8,128)S(1)}, u32[]{:S(2)}, u32[]{:S(2)}) %collective-permute-start.30) | collective-permute-done | bytes 163872 | tf_op jit(solution)/shard_map/ppermute | solution.py:14
  181.4 3.9 %collective-permute-start.32 = (f32[2,4,8,320]{3,2,1,0:T(8,128)S(1)}, f32[2,4,8,320]{3,2,1,0:T(8,128)S(1)}, u32[]{:S(2)}, u32[]{:S(2)}) collective-permute-start(f32[2,4,8,320]{3,2,1,0:T(8,128)S(1)} %get-tuple-element.240), channel_id=1, source_target_pairs={{0,4},{4,8},{8,12},{1,5},{5,9},{9,13},{2,6},{6,10},{10,14},{3,7},{... | collective-permute-start | bytes 245768 | tf_op jit(solution)/shard_map/ppermute | solution.py:14
  193.2 3.8 %collective-permute-done.34 = f32[2,16,4,320]{3,1,2,0:T(8,128)S(1)} collective-permute-done((f32[2,16,4,320]{3,1,2,0:T(8,128)S(1)}, f32[2,16,4,320]{3,1,2,0:T(8,128)S(1)}, u32[]{:S(2)}, u32[]{:S(2)}) %collective-permute-start.34) | collective-permute-done | bytes 163872 | tf_op jit(solution)/shard_map/ppermute | solution.py:14
  200.9 3.9 %collective-permute-start.36 = (f32[2,4,8,320]{3,2,1,0:T(8,128)S(1)}, f32[2,4,8,320]{3,2,1,0:T(8,128)S(1)}, u32[]{:S(2)}, u32[]{:S(2)}) collective-permute-start(f32[2,4,8,320]{3,2,1,0:T(8,128)S(1)} %get-tuple-element.238), channel_id=1, source_target_pairs={{0,4},{4,8},{8,12},{1,5},{5,9},{9,13},{2,6},{6,10},{10,14},{3,7},{... | collective-permute-start | bytes 245768 | tf_op jit(solution)/shard_map/ppermute | solution.py:14
  226.4 2.4 collective-permute-start.38
  229.7 3.6 %collective-permute-done.38 = f32[2,16,4,320]{3,1,2,0:T(8,128)S(1)} collective-permute-done((f32[2,16,4,320]{3,1,2,0:T(8,128)S(1)}, f32[2,16,4,320]{3,1,2,0:T(8,128)S(1)}, u32[]{:S(2)}, u32[]{:S(2)}) %collective-permute-start.38) | collective-permute-done | bytes 163872 | tf_op jit(solution)/shard_map/ppermute | solution.py:14
  236.7 7.0 %fusion.361 = (f32[8,8,320]{2,1,0:T(8,128)}, f32[8,8,320]{2,1,0:T(8,128)}) fusion(f32[8,8,320]{2,1,0:T(8,128)S(1)} %multiply_add_fusion.1, f32[8,8,320]{2,1,0:T(8,128)S(1)} %multiply_add_fusion.3, f32[8,8,320]{2,1,0:T(8,128)S(1)} %multiply_add_fusion.4, f32[8,8,320]{2,1,0:T(8,128)S(1)} %multiply_add_fusion.8, f32[8,8,320]{2,1,0:T(8,128)S(1)} %copy-done.7, ...), kind=kLoop, calls=%fused_computation.864 | loop fusion | flops 1228800 | bytes 1556530 | tf_op jit(solution)/shard_map/add | solution.py:119
  (239 shorter events, 98.2 us)
Async XLA Ops:
  1.5 23.6 %collective-permute-start.1 = (f32[2,4,8,320]{3,2,1,0:T(8,128)S(1)}, f32[2,4,8,320]{3,2,1,0:T(8,128)S(1)}, u32[]{:S(2)}, u32[]{:S(2)}) collective-permute-start(f32[2,4,8,320]{3,2,1,0:T(8,128)S(1)} %get-tuple-element.257), channel_id=1, source_target_pairs={{4,0},{8,4},{12,8},{5,1},{9,5},{13,9},{6,2},{10,6},{14,10},{7,3},{... | collective-permute-start | bytes 245768 | tf_op jit(solution)/shard_map/ppermute | solution.py:17
  3.9 21.3 %collective-permute-start = (f32[2,4,8,320]{3,2,1,0:T(8,128)S(1)}, f32[2,4,8,320]{3,2,1,0:T(8,128)S(1)}, u32[]{:S(2)}, u32[]{:S(2)}) collective-permute-start(f32[2,4,8,320]{3,2,1,0:T(8,128)S(1)} %get-tuple-element.256), channel_id=1, source_target_pairs={{0,4},{4,8},{8,12},{1,5},{5,9},{9,13},{2,6},{6,10},{10,14},{3,7},{... | collective-permute-start | bytes 245768 | tf_op jit(solution)/shard_map/ppermute | solution.py:14
  8.2 22.2 %all-to-all-start = ((f32[16,1,640]{2,1,0:T(1,128)}), f32[16,1,640]{2,1,0:T(1,128)S(1)}, u32[]{:S(2)}, u32[]{:S(2)}) async-start(f32[16,1,640]{2,1,0:T(1,128)} %reshape.617), calls=%async_computation | async-start | bytes 81920 | tf_op jit(solution)/shard_map/all_to_all | solution.py:70
  25.3 12.8 %collective-permute-start.3 = (f32[2,16,4,320]{3,1,2,0:T(8,128)S(1)}, f32[2,16,4,320]{3,1,2,0:T(8,128)S(1)}, u32[]{:S(2)}, u32[]{:S(2)}) collective-permute-start(f32[2,16,4,320]{3,1,2,0:T(8,128)S(1)} %copy.930), channel_id=1, source_target_pairs={{1,0},{2,1},{3,2},{5,4},{6,5},{7,6},{9,8},{10,9},{11,10},{13,12},{... | collective-permute-start | bytes 491528 | tf_op jit(solution)/shard_map/ppermute | solution.py:17
  27.3 11.0 %collective-permute-start.2 = (f32[2,16,4,320]{3,1,2,0:T(8,128)S(1)}, f32[2,16,4,320]{3,1,2,0:T(8,128)S(1)}, u32[]{:S(2)}, u32[]{:S(2)}) collective-permute-start(f32[2,16,4,320]{3,1,2,0:T(8,128)S(1)} %copy.929), channel_id=1, source_target_pairs={{0,1},{1,2},{2,3},{4,5},{5,6},{6,7},{8,9},{9,10},{10,11},{12,13},{... | collective-permute-start | bytes 491528 | tf_op jit(solution)/shard_map/ppermute | solution.py:14
  41.5 6.5 %collective-permute-start.5 = (f32[2,4,8,320]{3,2,1,0:T(8,128)S(1)}, f32[2,4,8,320]{3,2,1,0:T(8,128)S(1)}, u32[]{:S(2)}, u32[]{:S(2)}) collective-permute-start(f32[2,4,8,320]{3,2,1,0:T(8,128)S(1)} %get-tuple-element.255), channel_id=1, source_target_pairs={{4,0},{8,4},{12,8},{5,1},{9,5},{13,9},{6,2},{10,6},{14,10},{7,3},{... | collective-permute-start | bytes 245768 | tf_op jit(solution)/shard_map/ppermute | solution.py:17
  44.9 6.5 %collective-permute-start.4 = (f32[2,4,8,320]{3,2,1,0:T(8,128)S(1)}, f32[2,4,8,320]{3,2,1,0:T(8,128)S(1)}, u32[]{:S(2)}, u32[]{:S(2)}) collective-permute-start(f32[2,4,8,320]{3,2,1,0:T(8,128)S(1)} %get-tuple-element.254), channel_id=1, source_target_pairs={{0,4},{4,8},{8,12},{1,5},{5,9},{9,13},{2,6},{6,10},{10,14},{3,7},{... | collective-permute-start | bytes 245768 | tf_op jit(solution)/shard_map/ppermute | solution.py:14
  53.8 7.0 %collective-permute-start.6 = (f32[2,16,4,320]{3,1,2,0:T(8,128)S(1)}, f32[2,16,4,320]{3,1,2,0:T(8,128)S(1)}, u32[]{:S(2)}, u32[]{:S(2)}) collective-permute-start(f32[2,16,4,320]{3,1,2,0:T(8,128)S(1)} %copy.931), channel_id=1, source_target_pairs={{0,1},{1,2},{2,3},{4,5},{5,6},{6,7},{8,9},{9,10},{10,11},{12,13},{... | collective-permute-start | bytes 491528 | tf_op jit(solution)/shard_map/ppermute | solution.py:14
  62.5 6.5 %collective-permute-start.9 = (f32[2,4,8,320]{3,2,1,0:T(8,128)S(1)}, f32[2,4,8,320]{3,2,1,0:T(8,128)S(1)}, u32[]{:S(2)}, u32[]{:S(2)}) collective-permute-start(f32[2,4,8,320]{3,2,1,0:T(8,128)S(1)} %get-tuple-element.253), channel_id=1, source_target_pairs={{4,0},{8,4},{12,8},{5,1},{9,5},{13,9},{6,2},{10,6},{14,10},{7,3},{... | collective-permute-start | bytes 245768 | tf_op jit(solution)/shard_map/ppermute | solution.py:17
  66.0 6.5 %collective-permute-start.8 = (f32[2,4,8,320]{3,2,1,0:T(8,128)S(1)}, f32[2,4,8,320]{3,2,1,0:T(8,128)S(1)}, u32[]{:S(2)}, u32[]{:S(2)}) collective-permute-start(f32[2,4,8,320]{3,2,1,0:T(8,128)S(1)} %get-tuple-element.252), channel_id=1, source_target_pairs={{0,4},{4,8},{8,12},{1,5},{5,9},{9,13},{2,6},{6,10},{10,14},{3,7},{... | collective-permute-start | bytes 245768 | tf_op jit(solution)/shard_map/ppermute | solution.py:14
  74.6 7.0 %collective-permute-start.10 = (f32[2,16,4,320]{3,1,2,0:T(8,128)S(1)}, f32[2,16,4,320]{3,1,2,0:T(8,128)S(1)}, u32[]{:S(2)}, u32[]{:S(2)}) collective-permute-start(f32[2,16,4,320]{3,1,2,0:T(8,128)S(1)} %copy.933), channel_id=1, source_target_pairs={{0,1},{1,2},{2,3},{4,5},{5,6},{6,7},{8,9},{9,10},{10,11},{12,13},{... | collective-permute-start | bytes 491528 | tf_op jit(solution)/shard_map/ppermute | solution.py:14
  83.3 6.5 %collective-permute-start.13 = (f32[2,4,8,320]{3,2,1,0:T(8,128)S(1)}, f32[2,4,8,320]{3,2,1,0:T(8,128)S(1)}, u32[]{:S(2)}, u32[]{:S(2)}) collective-permute-start(f32[2,4,8,320]{3,2,1,0:T(8,128)S(1)} %get-tuple-element.251), channel_id=1, source_target_pairs={{4,0},{8,4},{12,8},{5,1},{9,5},{13,9},{6,2},{10,6},{14,10},{7,3},{... | collective-permute-start | bytes 245768 | tf_op jit(solution)/shard_map/ppermute | solution.py:17
  85.2 6.5 %collective-permute-start.12 = (f32[2,4,8,320]{3,2,1,0:T(8,128)S(1)}, f32[2,4,8,320]{3,2,1,0:T(8,128)S(1)}, u32[]{:S(2)}, u32[]{:S(2)}) collective-permute-start(f32[2,4,8,320]{3,2,1,0:T(8,128)S(1)} %get-tuple-element.250), channel_id=1, source_target_pairs={{0,4},{4,8},{8,12},{1,5},{5,9},{9,13},{2,6},{6,10},{10,14},{3,7},{... | collective-permute-start | bytes 245768 | tf_op jit(solution)/shard_map/ppermute | solution.py:14
  93.8 7.0 %collective-permute-start.14 = (f32[2,16,4,320]{3,1,2,0:T(8,128)S(1)}, f32[2,16,4,320]{3,1,2,0:T(8,128)S(1)}, u32[]{:S(2)}, u32[]{:S(2)}) collective-permute-start(f32[2,16,4,320]{3,1,2,0:T(8,128)S(1)} %copy.935), channel_id=1, source_target_pairs={{0,1},{1,2},{2,3},{4,5},{5,6},{6,7},{8,9},{9,10},{10,11},{12,13},{... | collective-permute-start | bytes 491528 | tf_op jit(solution)/shard_map/ppermute | solution.py:14
  102.4 6.5 %collective-permute-start.17 = (f32[2,4,8,320]{3,2,1,0:T(8,128)S(1)}, f32[2,4,8,320]{3,2,1,0:T(8,128)S(1)}, u32[]{:S(2)}, u32[]{:S(2)}) collective-permute-start(f32[2,4,8,320]{3,2,1,0:T(8,128)S(1)} %get-tuple-element.249), channel_id=1, source_target_pairs={{4,0},{8,4},{12,8},{5,1},{9,5},{13,9},{6,2},{10,6},{14,10},{7,3},{... | collective-permute-start | bytes 245768 | tf_op jit(solution)/shard_map/ppermute | solution.py:17
  104.4 6.5 %collective-permute-start.16 = (f32[2,4,8,320]{3,2,1,0:T(8,128)S(1)}, f32[2,4,8,320]{3,2,1,0:T(8,128)S(1)}, u32[]{:S(2)}, u32[]{:S(2)}) collective-permute-start(f32[2,4,8,320]{3,2,1,0:T(8,128)S(1)} %get-tuple-element.248), channel_id=1, source_target_pairs={{0,4},{4,8},{8,12},{1,5},{5,9},{9,13},{2,6},{6,10},{10,14},{3,7},{... | collective-permute-start | bytes 245768 | tf_op jit(solution)/shard_map/ppermute | solution.py:14
  113.0 7.0 %collective-permute-start.18 = (f32[2,16,4,320]{3,1,2,0:T(8,128)S(1)}, f32[2,16,4,320]{3,1,2,0:T(8,128)S(1)}, u32[]{:S(2)}, u32[]{:S(2)}) collective-permute-start(f32[2,16,4,320]{3,1,2,0:T(8,128)S(1)} %copy.937), channel_id=1, source_target_pairs={{0,1},{1,2},{2,3},{4,5},{5,6},{6,7},{8,9},{9,10},{10,11},{12,13},{... | collective-permute-start | bytes 491528 | tf_op jit(solution)/shard_map/ppermute | solution.py:14
  121.7 6.5 %collective-permute-start.21 = (f32[2,4,8,320]{3,2,1,0:T(8,128)S(1)}, f32[2,4,8,320]{3,2,1,0:T(8,128)S(1)}, u32[]{:S(2)}, u32[]{:S(2)}) collective-permute-start(f32[2,4,8,320]{3,2,1,0:T(8,128)S(1)} %get-tuple-element.247), channel_id=1, source_target_pairs={{4,0},{8,4},{12,8},{5,1},{9,5},{13,9},{6,2},{10,6},{14,10},{7,3},{... | collective-permute-start | bytes 245768 | tf_op jit(solution)/shard_map/ppermute | solution.py:17
  123.6 6.5 %collective-permute-start.20 = (f32[2,4,8,320]{3,2,1,0:T(8,128)S(1)}, f32[2,4,8,320]{3,2,1,0:T(8,128)S(1)}, u32[]{:S(2)}, u32[]{:S(2)}) collective-permute-start(f32[2,4,8,320]{3,2,1,0:T(8,128)S(1)} %get-tuple-element.246), channel_id=1, source_target_pairs={{0,4},{4,8},{8,12},{1,5},{5,9},{9,13},{2,6},{6,10},{10,14},{3,7},{... | collective-permute-start | bytes 245768 | tf_op jit(solution)/shard_map/ppermute | solution.py:14
  132.2 7.0 %collective-permute-start.22 = (f32[2,16,4,320]{3,1,2,0:T(8,128)S(1)}, f32[2,16,4,320]{3,1,2,0:T(8,128)S(1)}, u32[]{:S(2)}, u32[]{:S(2)}) collective-permute-start(f32[2,16,4,320]{3,1,2,0:T(8,128)S(1)} %copy.939), channel_id=1, source_target_pairs={{0,1},{1,2},{2,3},{4,5},{5,6},{6,7},{8,9},{9,10},{10,11},{12,13},{... | collective-permute-start | bytes 491528 | tf_op jit(solution)/shard_map/ppermute | solution.py:14
  141.0 6.5 %collective-permute-start.25 = (f32[2,4,8,320]{3,2,1,0:T(8,128)S(1)}, f32[2,4,8,320]{3,2,1,0:T(8,128)S(1)}, u32[]{:S(2)}, u32[]{:S(2)}) collective-permute-start(f32[2,4,8,320]{3,2,1,0:T(8,128)S(1)} %get-tuple-element.245), channel_id=1, source_target_pairs={{4,0},{8,4},{12,8},{5,1},{9,5},{13,9},{6,2},{10,6},{14,10},{7,3},{... | collective-permute-start | bytes 245768 | tf_op jit(solution)/shard_map/ppermute | solution.py:17
  142.9 6.5 %collective-permute-start.24 = (f32[2,4,8,320]{3,2,1,0:T(8,128)S(1)}, f32[2,4,8,320]{3,2,1,0:T(8,128)S(1)}, u32[]{:S(2)}, u32[]{:S(2)}) collective-permute-start(f32[2,4,8,320]{3,2,1,0:T(8,128)S(1)} %get-tuple-element.244), channel_id=1, source_target_pairs={{0,4},{4,8},{8,12},{1,5},{5,9},{9,13},{2,6},{6,10},{10,14},{3,7},{... | collective-permute-start | bytes 245768 | tf_op jit(solution)/shard_map/ppermute | solution.py:14
  151.5 7.0 %collective-permute-start.26 = (f32[2,16,4,320]{3,1,2,0:T(8,128)S(1)}, f32[2,16,4,320]{3,1,2,0:T(8,128)S(1)}, u32[]{:S(2)}, u32[]{:S(2)}) collective-permute-start(f32[2,16,4,320]{3,1,2,0:T(8,128)S(1)} %copy.941), channel_id=1, source_target_pairs={{0,1},{1,2},{2,3},{4,5},{5,6},{6,7},{8,9},{9,10},{10,11},{12,13},{... | collective-permute-start | bytes 491528 | tf_op jit(solution)/shard_map/ppermute | solution.py:14
  160.3 6.5 %collective-permute-start.29 = (f32[2,4,8,320]{3,2,1,0:T(8,128)S(1)}, f32[2,4,8,320]{3,2,1,0:T(8,128)S(1)}, u32[]{:S(2)}, u32[]{:S(2)}) collective-permute-start(f32[2,4,8,320]{3,2,1,0:T(8,128)S(1)} %get-tuple-element.243), channel_id=1, source_target_pairs={{4,0},{8,4},{12,8},{5,1},{9,5},{13,9},{6,2},{10,6},{14,10},{7,3},{... | collective-permute-start | bytes 245768 | tf_op jit(solution)/shard_map/ppermute | solution.py:17
  162.2 6.5 %collective-permute-start.28 = (f32[2,4,8,320]{3,2,1,0:T(8,128)S(1)}, f32[2,4,8,320]{3,2,1,0:T(8,128)S(1)}, u32[]{:S(2)}, u32[]{:S(2)}) collective-permute-start(f32[2,4,8,320]{3,2,1,0:T(8,128)S(1)} %get-tuple-element.242), channel_id=1, source_target_pairs={{0,4},{4,8},{8,12},{1,5},{5,9},{9,13},{2,6},{6,10},{10,14},{3,7},{... | collective-permute-start | bytes 245768 | tf_op jit(solution)/shard_map/ppermute | solution.py:14
  170.8 7.0 %collective-permute-start.30 = (f32[2,16,4,320]{3,1,2,0:T(8,128)S(1)}, f32[2,16,4,320]{3,1,2,0:T(8,128)S(1)}, u32[]{:S(2)}, u32[]{:S(2)}) collective-permute-start(f32[2,16,4,320]{3,1,2,0:T(8,128)S(1)} %copy.943), channel_id=1, source_target_pairs={{0,1},{1,2},{2,3},{4,5},{5,6},{6,7},{8,9},{9,10},{10,11},{12,13},{... | collective-permute-start | bytes 491528 | tf_op jit(solution)/shard_map/ppermute | solution.py:14
  179.5 6.5 %collective-permute-start.33 = (f32[2,4,8,320]{3,2,1,0:T(8,128)S(1)}, f32[2,4,8,320]{3,2,1,0:T(8,128)S(1)}, u32[]{:S(2)}, u32[]{:S(2)}) collective-permute-start(f32[2,4,8,320]{3,2,1,0:T(8,128)S(1)} %get-tuple-element.241), channel_id=1, source_target_pairs={{4,0},{8,4},{12,8},{5,1},{9,5},{13,9},{6,2},{10,6},{14,10},{7,3},{... | collective-permute-start | bytes 245768 | tf_op jit(solution)/shard_map/ppermute | solution.py:17
  181.4 6.5 %collective-permute-start.32 = (f32[2,4,8,320]{3,2,1,0:T(8,128)S(1)}, f32[2,4,8,320]{3,2,1,0:T(8,128)S(1)}, u32[]{:S(2)}, u32[]{:S(2)}) collective-permute-start(f32[2,4,8,320]{3,2,1,0:T(8,128)S(1)} %get-tuple-element.240), channel_id=1, source_target_pairs={{0,4},{4,8},{8,12},{1,5},{5,9},{9,13},{2,6},{6,10},{10,14},{3,7},{... | collective-permute-start | bytes 245768 | tf_op jit(solution)/shard_map/ppermute | solution.py:14
  190.0 7.0 %collective-permute-start.34 = (f32[2,16,4,320]{3,1,2,0:T(8,128)S(1)}, f32[2,16,4,320]{3,1,2,0:T(8,128)S(1)}, u32[]{:S(2)}, u32[]{:S(2)}) collective-permute-start(f32[2,16,4,320]{3,1,2,0:T(8,128)S(1)} %copy.945), channel_id=1, source_target_pairs={{0,1},{1,2},{2,3},{4,5},{5,6},{6,7},{8,9},{9,10},{10,11},{12,13},{... | collective-permute-start | bytes 491528 | tf_op jit(solution)/shard_map/ppermute | solution.py:14
  198.8 25.5 %collective-permute-start.37 = (f32[2,4,8,320]{3,2,1,0:T(8,128)S(1)}, f32[2,4,8,320]{3,2,1,0:T(8,128)S(1)}, u32[]{:S(2)}, u32[]{:S(2)}) collective-permute-start(f32[2,4,8,320]{3,2,1,0:T(8,128)S(1)} %get-tuple-element.239), channel_id=1, source_target_pairs={{4,0},{8,4},{12,8},{5,1},{9,5},{13,9},{6,2},{10,6},{14,10},{7,3},{... | collective-permute-start | bytes 245768 | tf_op jit(solution)/shard_map/ppermute | solution.py:17
  200.9 23.5 %collective-permute-start.36 = (f32[2,4,8,320]{3,2,1,0:T(8,128)S(1)}, f32[2,4,8,320]{3,2,1,0:T(8,128)S(1)}, u32[]{:S(2)}, u32[]{:S(2)}) collective-permute-start(f32[2,4,8,320]{3,2,1,0:T(8,128)S(1)} %get-tuple-element.238), channel_id=1, source_target_pairs={{0,4},{4,8},{8,12},{1,5},{5,9},{9,13},{2,6},{6,10},{10,14},{3,7},{... | collective-permute-start | bytes 245768 | tf_op jit(solution)/shard_map/ppermute | solution.py:14
  226.4 7.0 %collective-permute-start.38 = (f32[2,16,4,320]{3,1,2,0:T(8,128)S(1)}, f32[2,16,4,320]{3,1,2,0:T(8,128)S(1)}, u32[]{:S(2)}, u32[]{:S(2)}) collective-permute-start(f32[2,16,4,320]{3,1,2,0:T(8,128)S(1)} %copy.947), channel_id=1, source_target_pairs={{0,1},{1,2},{2,3},{4,5},{5,6},{6,7},{8,9},{9,10},{10,11},{12,13},{... | collective-permute-start | bytes 491528 | tf_op jit(solution)/shard_map/ppermute | solution.py:14
  (23 other events, 188.9 us)
